TPU v7x, 32 devices: a whole 2x2x4 slice. The times are simulated.
32 devices in a mesh: wide: 8 (over z, x), narrow: 4 (over y, core).
Axes of the slice: x: 2, y: 2, z: 4, core: 2. Of those that a mesh axis runs over, the one named last changes fastest.
Arguments:
- samples: bfloat16 [16384, 1024], P(('wide', 'narrow')), may hold values from -16 to 16
- centroid_table: bfloat16 [16384, 1024], P('wide', 'narrow'), may hold values from -6 to 6
- owner: int32 [16384], replicated, may hold values from 0 to 7, as said below
- slot: int32 [16384], replicated, may hold values from 0 to 2047, as said below
- assign: int32 [16384], P('wide'), may hold values from 0 to 16383, as said below
- codebook: float32 [8, 2048, 128], P('narrow'), may hold values from -16 to 16
Outputs:
- residual: bfloat16 [16384, 1024], P('wide', 'narrow')
- refined: float32 [8, 2048, 128], P('narrow')
Inputs may be any that keep to these rules, and one draw needn't show every extreme that they name: owner and slot give each coarse centroid a distinct storage position owner * 2048 + slot. `slot`: see owner. `assign`: in each aligned block of 2048 rows (the rows of one index of wide), at most 512 rows have centroids with one owner, and some owner has exactly 512.
All inputs are finite; a program needn't handle non-finite values.
Results may differ from a plain program's by a relative error of at most 0.0079.
Values may be sent and summed in bfloat16 or wider, within the bound.
No kernel may reach another device: no remote copies, remote signals or barrier semaphores. Data moves between devices by JAX's collectives and lax.ppermute only.
A program may use at most 64 MiB of HBM per device.

v0:
```python
import jax
import jax.numpy as jnp
from jax import lax
from jax.sharding import PartitionSpec as P

ITERS = 2
softness_level = 16.0
prior_weight = 1.0


def score_pass(blocks, narrow_words, codeword_norm_values):
    spaces = narrow_words.shape[0]
    words_count = narrow_words.shape[1]
    sub_width = narrow_words.shape[2]

    def block_step(running, row_block):
        inner_product_rows = jnp.einsum(
            "bms,mks->mbk", row_block, narrow_words, preferred_element_type=jnp.float32
        )
        score_matrix = (
            2.0 * inner_product_rows - codeword_norm_values[:, None, :]
        ) / softness_level
        weights_soft = jax.nn.softmax(score_matrix, axis=2).astype(jnp.bfloat16)
        totals = running[0] + jnp.einsum(
            "mbk,bms->mks", weights_soft, row_block, preferred_element_type=jnp.float32
        )
        return ((totals, running[1] + jnp.sum(weights_soft, axis=1, dtype=jnp.float32)), None)

    start = (
        jnp.zeros((spaces, words_count, sub_width), jnp.float32),
        jnp.zeros((spaces, words_count), jnp.float32),
    )
    (totals, counts), ignored = lax.scan(block_step, start, blocks)
    return (totals, counts)


def on_device(samples, centroid_table, owner, slot, assign, codebook):
    regrouped = lax.all_to_all(samples, "narrow", split_axis=1, concat_axis=0, tiled=True)
    group_rows = regrouped.shape[0]
    owner_of = owner[assign]
    slot_of = slot[assign]
    whole = lax.all_gather(centroid_table, "wide", axis=0, tiled=True)
    centre = jnp.take(whole, owner_of * centroid_table.shape[0] + slot_of, axis=0)
    residual = (regrouped.astype(jnp.float32) - centre.astype(jnp.float32)).astype(jnp.bfloat16)
    spaces = codebook.shape[0]
    sub_width = codebook.shape[2]
    block_size = 512
    blocks = residual.reshape(group_rows // block_size, block_size, spaces, sub_width)
    codewords = codebook
    narrow_words = codebook.astype(jnp.bfloat16)
    codeword_norm_values = jnp.sum(codebook * codebook, axis=2)
    for iteration in range(ITERS):
        narrow_words = codewords.astype(jnp.bfloat16)
        codeword_norm_values = jnp.sum(codewords * codewords, axis=2)
        totals, counts = score_pass(blocks, narrow_words, codeword_norm_values)
        totals, counts = lax.psum((totals, counts), "wide")
        codewords = (totals + prior_weight * codewords) / (counts[:, :, None] + prior_weight)
    return (residual, codewords)


def solution(mesh):
    return jax.shard_map(
        on_device,
        mesh=mesh,
        in_specs=(
            P(("wide", "narrow"), None),
            P("wide", "narrow"),
            P(),
            P(),
            P("wide"),
            P("narrow", None, None),
        ),
        out_specs=(P("wide", "narrow"), P("narrow", None, None)),
        check_vma=False,
    )
```

profile of v0, /device:TPU:0, one launch (start us, length us, event | category | flops | bytes accessed | tf_op | source)
XLA Modules:
  0.0 518.3 jit_solution(10853874548214603583)
XLA Ops:
  7.9 2.3 copy.14
  10.2 4.3 all-to-all-start
  14.5 11.8 %gather_fusion.1 = s32[2048]{0:T(1024)S(1)} fusion(s32[16384]{0:T(1024)S(1)} %copy-done, s32[2048]{0:T(1024)S(1)} %fusion.55), kind=kCustom, calls=%fused_computation.1 | custom fusion | bytes 24576 | tf_op jit(solution)/shard_map/gather | solution.py:41
  26.3 11.8 %gather_fusion = s32[2048]{0:T(1024)S(1)} fusion(s32[16384]{0:T(1024)S(1)} %copy-done.2, s32[2048]{0:T(1024)S(1)} %fusion.55), kind=kCustom, calls=%fused_computation | custom fusion | bytes 24576 | tf_op jit(solution)/shard_map/gather | solution.py:40
  38.2 3.9 multiply_reduce_fusion.1
  42.1 2.6 fusion.66
  44.7 92.6 %all-gather.2.cloned.1.call-done = bf16[16384,256]{1,0:T(8,128)(2,1)} async-done(((bf16[2048,256]{1,0:T(8,128)(2,1)}), bf16[16384,256]{1,0:T(8,128)(2,1)}) %all-gather.2.cloned.1.call-update) | async-done | bytes 8388624 | tf_op jit(solution)/shard_map/all_gather | solution.py:42
  137.4 11.1 %gather_fusion.2 = bf16[2048,256]{1,0:T(8,128)(2,1)S(1)} fusion(bf16[16384,256]{1,0:T(8,128)(2,1)} %all-gather.2.cloned.1.call-done, s32[2048]{0:T(1024)S(1)} %broadcast_clamp_fusion), kind=kCustom, calls=%fused_computation.2 | custom fusion | bytes 2105344 | tf_op jit(solution)/shard_map/jit(_take)/gather | solution.py:43
  148.5 1.4 gather.15
  149.8 3.7 copy.16
  153.5 3.3 subtract_convert_fusion
  156.8 1.6 copy.18
  158.4 69.5 %while.26 = (s32[]{:T(128)}, f32[2,2048,128]{2,1,0:T(8,128)S(1)}, f32[2,2048]{1,0:T(2,128)S(1)}, bf16[4,512,2,128]{3,1,2,0:T(8,128)(2,1)S(1)}, bf16[2,2048,128]{...) while((s32[]{:T(128)}, f32[2,2048,128]{2,1,0:T(8,128)S(1)}, ...), condition=%wide.region_5.6_spmd.clone, body=%wide.region_1.5_spmd.clone.sunk | while | flops 1093670912 | bytes 31023212 | solution.py:33
  158.4 7.2 %fusion.87 = (f32[2,512]{1,0:T(2,128)S(1)}, f32[2,512,2048]{2,1,0:T(8,128)}) fusion(f32[2,2048]{1,0:T(2,128)S(1)} %get-tuple-element.277, bf16[2,2048,128]{2,1,0:T(8,128)(2,1)} %get-tuple-element.276, bf16[4,512,2,128]{3,1,2,0:T(8,128)(2,1)S(1)} %get-tuple-element.275, s32[]{:T(128)S(6)} %copy.24), kind=kOutput, calls=%fused_computation.70.clone.1 | convolution fusion | flops 547358720 | bytes 9719812 | tf_op jit(solution)/shard_map/while/body/eval_jaxpr/sub | solution.py:23
  165.6 5.5 %convert_reduce_fusion.4 = (f32[2,2048]{1,0:T(2,128)S(1)}, bf16[2,512,2048]{2,1,0:T(8,128)(2,1)}) fusion(f32[2,512,2048]{2,1,0:T(8,128)} %get-tuple-element.242, f32[2,512]{1,0:T(2,128)S(1)} %get-tuple-element.243), kind=kLoop, calls=%fused_computation.4.clone.1 | loop fusion | flops 8384512 | bytes 12603392 | tf_op jit(solution)/shard_map/while/body/eval_jaxpr/reduce_sum | solution.py:27
  171.1 4.7 convolution_add_fusion.4
  175.8 7.2 %fusion.87 = (f32[2,512]{1,0:T(2,128)S(1)}, f32[2,512,2048]{2,1,0:T(8,128)}) fusion(f32[2,2048]{1,0:T(2,128)S(1)} %get-tuple-element.277, bf16[2,2048,128]{2,1,0:T(8,128)(2,1)} %get-tuple-element.276, bf16[4,512,2,128]{3,1,2,0:T(8,128)(2,1)S(1)} %get-tuple-element.275, s32[]{:T(128)S(6)} %copy.24), kind=kOutput, calls=%fused_computation.70.clone.1 | convolution fusion | flops 547358720 | bytes 9719812 | tf_op jit(solution)/shard_map/while/body/eval_jaxpr/sub | solution.py:23
  183.0 5.5 %convert_reduce_fusion.4 = (f32[2,2048]{1,0:T(2,128)S(1)}, bf16[2,512,2048]{2,1,0:T(8,128)(2,1)}) fusion(f32[2,512,2048]{2,1,0:T(8,128)} %get-tuple-element.242, f32[2,512]{1,0:T(2,128)S(1)} %get-tuple-element.243), kind=kLoop, calls=%fused_computation.4.clone.1 | loop fusion | flops 8384512 | bytes 12603392 | tf_op jit(solution)/shard_map/while/body/eval_jaxpr/reduce_sum | solution.py:27
  188.5 4.7 convolution_add_fusion.4
  193.2 7.2 %fusion.87 = (f32[2,512]{1,0:T(2,128)S(1)}, f32[2,512,2048]{2,1,0:T(8,128)}) fusion(f32[2,2048]{1,0:T(2,128)S(1)} %get-tuple-element.277, bf16[2,2048,128]{2,1,0:T(8,128)(2,1)} %get-tuple-element.276, bf16[4,512,2,128]{3,1,2,0:T(8,128)(2,1)S(1)} %get-tuple-element.275, s32[]{:T(128)S(6)} %copy.24), kind=kOutput, calls=%fused_computation.70.clone.1 | convolution fusion | flops 547358720 | bytes 9719812 | tf_op jit(solution)/shard_map/while/body/eval_jaxpr/sub | solution.py:23
  200.3 5.5 %convert_reduce_fusion.4 = (f32[2,2048]{1,0:T(2,128)S(1)}, bf16[2,512,2048]{2,1,0:T(8,128)(2,1)}) fusion(f32[2,512,2048]{2,1,0:T(8,128)} %get-tuple-element.242, f32[2,512]{1,0:T(2,128)S(1)} %get-tuple-element.243), kind=kLoop, calls=%fused_computation.4.clone.1 | loop fusion | flops 8384512 | bytes 12603392 | tf_op jit(solution)/shard_map/while/body/eval_jaxpr/reduce_sum | solution.py:27
  205.9 4.7 convolution_add_fusion.4
  210.6 7.2 %fusion.87 = (f32[2,512]{1,0:T(2,128)S(1)}, f32[2,512,2048]{2,1,0:T(8,128)}) fusion(f32[2,2048]{1,0:T(2,128)S(1)} %get-tuple-element.277, bf16[2,2048,128]{2,1,0:T(8,128)(2,1)} %get-tuple-element.276, bf16[4,512,2,128]{3,1,2,0:T(8,128)(2,1)S(1)} %get-tuple-element.275, s32[]{:T(128)S(6)} %copy.24), kind=kOutput, calls=%fused_computation.70.clone.1 | convolution fusion | flops 547358720 | bytes 9719812 | tf_op jit(solution)/shard_map/while/body/eval_jaxpr/sub | solution.py:23
  217.7 5.5 %convert_reduce_fusion.4 = (f32[2,2048]{1,0:T(2,128)S(1)}, bf16[2,512,2048]{2,1,0:T(8,128)(2,1)}) fusion(f32[2,512,2048]{2,1,0:T(8,128)} %get-tuple-element.242, f32[2,512]{1,0:T(2,128)S(1)} %get-tuple-element.243), kind=kLoop, calls=%fused_computation.4.clone.1 | loop fusion | flops 8384512 | bytes 12603392 | tf_op jit(solution)/shard_map/while/body/eval_jaxpr/reduce_sum | solution.py:27
  223.2 4.7 convolution_add_fusion.4
  228.0 1.3 copy-done.3
  229.4 35.4 %psum.29 = f32[2,2048]{1,0:T(2,128)S(1)} all-reduce(f32[2,2048]{1,0:T(2,128)S(1)} %get-tuple-element.69), channel_id=1, replica_groups=mesh['wide'=8,'narrow'=4] {'wide'}, use_global_device_ids=true, to_apply=%region_7.8 | all-reduce | flops 4096 | bytes 32768 | tf_op jit(solution)/shard_map/psum | solution.py:56
  264.8 65.7 %all-reduce.3.cloned.1.call-done = f32[2,2048,128]{2,1,0:T(8,128)} async-done(((f32[2,2048,128]{2,1,0:T(8,128)}), f32[2,2048,128]{2,1,0:T(8,128)}) %all-reduce.3.cloned.1.call-update) | async-done | bytes 2097168 | tf_op jit(solution)/shard_map/psum | solution.py:56
  330.5 2.9 multiply_reduce_fusion
  333.4 1.3 copy-done.5
  335.8 69.5 %while.27 = (s32[]{:T(128)}, f32[2,2048,128]{2,1,0:T(8,128)S(1)}, f32[2,2048]{1,0:T(2,128)S(1)}, bf16[4,512,2,128]{3,1,2,0:T(8,128)(2,1)S(1)}, bf16[2,2048,128]{...) while((s32[]{:T(128)}, f32[2,2048,128]{2,1,0:T(8,128)S(1)}, ...), condition=%wide.region_13.14_spmd.clone, body=%wide.region_9.0_spmd.clone.sunk | while | flops 1093670912 | bytes 31023212 | solution.py:33
  335.8 7.1 %fusion.92 = (f32[2,512]{1,0:T(2,128)S(1)}, f32[2,512,2048]{2,1,0:T(8,128)}) fusion(f32[2,2048]{1,0:T(2,128)S(1)} %get-tuple-element.301, bf16[2,2048,128]{2,1,0:T(8,128)(2,1)} %get-tuple-element.300, bf16[4,512,2,128]{3,1,2,0:T(8,128)(2,1)S(1)} %get-tuple-element.299, s32[]{:T(128)S(6)} %copy.34), kind=kOutput, calls=%fused_computation.71.clone.1 | convolution fusion | flops 547358720 | bytes 9719812 | tf_op jit(solution)/shard_map/while/body/eval_jaxpr/sub | solution.py:23
  342.9 5.5 %convert_reduce_fusion.5 = (f32[2,2048]{1,0:T(2,128)S(1)}, bf16[2,512,2048]{2,1,0:T(8,128)(2,1)}) fusion(f32[2,512,2048]{2,1,0:T(8,128)} %get-tuple-element.252, f32[2,512]{1,0:T(2,128)S(1)} %get-tuple-element.253), kind=kLoop, calls=%fused_computation.28.clone.1 | loop fusion | flops 8384512 | bytes 12603392 | tf_op jit(solution)/shard_map/while/body/eval_jaxpr/reduce_sum | solution.py:27
  348.4 4.7 convolution_add_fusion.5
  353.2 7.2 %fusion.92 = (f32[2,512]{1,0:T(2,128)S(1)}, f32[2,512,2048]{2,1,0:T(8,128)}) fusion(f32[2,2048]{1,0:T(2,128)S(1)} %get-tuple-element.301, bf16[2,2048,128]{2,1,0:T(8,128)(2,1)} %get-tuple-element.300, bf16[4,512,2,128]{3,1,2,0:T(8,128)(2,1)S(1)} %get-tuple-element.299, s32[]{:T(128)S(6)} %copy.34), kind=kOutput, calls=%fused_computation.71.clone.1 | convolution fusion | flops 547358720 | bytes 9719812 | tf_op jit(solution)/shard_map/while/body/eval_jaxpr/sub | solution.py:23
  360.3 5.5 %convert_reduce_fusion.5 = (f32[2,2048]{1,0:T(2,128)S(1)}, bf16[2,512,2048]{2,1,0:T(8,128)(2,1)}) fusion(f32[2,512,2048]{2,1,0:T(8,128)} %get-tuple-element.252, f32[2,512]{1,0:T(2,128)S(1)} %get-tuple-element.253), kind=kLoop, calls=%fused_computation.28.clone.1 | loop fusion | flops 8384512 | bytes 12603392 | tf_op jit(solution)/shard_map/while/body/eval_jaxpr/reduce_sum | solution.py:27
  365.8 4.7 convolution_add_fusion.5
  370.5 7.2 %fusion.92 = (f32[2,512]{1,0:T(2,128)S(1)}, f32[2,512,2048]{2,1,0:T(8,128)}) fusion(f32[2,2048]{1,0:T(2,128)S(1)} %get-tuple-element.301, bf16[2,2048,128]{2,1,0:T(8,128)(2,1)} %get-tuple-element.300, bf16[4,512,2,128]{3,1,2,0:T(8,128)(2,1)S(1)} %get-tuple-element.299, s32[]{:T(128)S(6)} %copy.34), kind=kOutput, calls=%fused_computation.71.clone.1 | convolution fusion | flops 547358720 | bytes 9719812 | tf_op jit(solution)/shard_map/while/body/eval_jaxpr/sub | solution.py:23
  377.7 5.5 %convert_reduce_fusion.5 = (f32[2,2048]{1,0:T(2,128)S(1)}, bf16[2,512,2048]{2,1,0:T(8,128)(2,1)}) fusion(f32[2,512,2048]{2,1,0:T(8,128)} %get-tuple-element.252, f32[2,512]{1,0:T(2,128)S(1)} %get-tuple-element.253), kind=kLoop, calls=%fused_computation.28.clone.1 | loop fusion | flops 8384512 | bytes 12603392 | tf_op jit(solution)/shard_map/while/body/eval_jaxpr/reduce_sum | solution.py:27
  383.2 4.7 convolution_add_fusion.5
  387.9 7.2 %fusion.92 = (f32[2,512]{1,0:T(2,128)S(1)}, f32[2,512,2048]{2,1,0:T(8,128)}) fusion(f32[2,2048]{1,0:T(2,128)S(1)} %get-tuple-element.301, bf16[2,2048,128]{2,1,0:T(8,128)(2,1)} %get-tuple-element.300, bf16[4,512,2,128]{3,1,2,0:T(8,128)(2,1)S(1)} %get-tuple-element.299, s32[]{:T(128)S(6)} %copy.34), kind=kOutput, calls=%fused_computation.71.clone.1 | convolution fusion | flops 547358720 | bytes 9719812 | tf_op jit(solution)/shard_map/while/body/eval_jaxpr/sub | solution.py:23
  395.1 5.5 %convert_reduce_fusion.5 = (f32[2,2048]{1,0:T(2,128)S(1)}, bf16[2,512,2048]{2,1,0:T(8,128)(2,1)}) fusion(f32[2,512,2048]{2,1,0:T(8,128)} %get-tuple-element.252, f32[2,512]{1,0:T(2,128)S(1)} %get-tuple-element.253), kind=kLoop, calls=%fused_computation.28.clone.1 | loop fusion | flops 8384512 | bytes 12603392 | tf_op jit(solution)/shard_map/while/body/eval_jaxpr/reduce_sum | solution.py:27
  400.6 4.7 convolution_add_fusion.5
  406.6 3.0 copy.15
  409.6 2.7 fusion.54
  412.3 36.7 %psum.31 = f32[2,2048]{1,0:T(2,128)S(1)} all-reduce(f32[2,2048]{1,0:T(2,128)S(1)} %get-tuple-element.71), channel_id=1, replica_groups=mesh['wide'=8,'narrow'=4] {'wide'}, use_global_device_ids=true, to_apply=%region_15.16 | all-reduce | flops 4096 | bytes 32768 | tf_op jit(solution)/shard_map/psum | solution.py:56
  449.0 59.9 %all-reduce.5.cloned.1.call-done = f32[2,2048,128]{2,1,0:T(8,128)} async-done(((f32[2,2048,128]{2,1,0:T(8,128)}), f32[2,2048,128]{2,1,0:T(8,128)}) %all-reduce.5.cloned.1.call-update) | async-done | bytes 2097168 | tf_op jit(solution)/shard_map/psum | solution.py:56
  508.9 2.9 add_divide_fusion
  (46 shorter events, 3.5 us)
Async XLA Ops:
  7.2 7.3 %copy-start = (s32[16384]{0:T(1024)S(1)}, s32[16384]{0:T(1024)}, u32[]{:S(2)}) copy-start(s32[16384]{0:T(1024)} %param.13) | copy-start | bytes 196612
  7.2 130.2 %all-gather.2.cloned.1.call-start = ((), (), s32[]{:S(2)}) async-start(), calls=%async_computation.1 | async-start | bytes 9437184 | tf_op jit(solution)/shard_map/all_gather | solution.py:42
  7.9 6.6 %copy-start.9 = (s32[2048]{0:T(1024)S(1)}, s32[2048]{0:T(1024)}, u32[]{:S(2)}) copy-start(s32[2048]{0:T(1024)} %param.14) | copy-start | bytes 24580
  10.2 31.9 %all-to-all-start = ((bf16[512,4,256]{0,2,1:T(8,128)(2,1)}), bf16[512,4,256]{0,2,1:T(8,128)(2,1)S(1)}, u32[]{:S(2)}, u32[]{:S(2)}) async-start(bf16[512,4,256]{0,2,1:T(8,128)(2,1)} %bitcast), calls=%async_computation | async-start | bytes 2097152 | tf_op jit(solution)/shard_map/all_to_all | solution.py:38
  14.5 316.0 %all-reduce.3.cloned.1.call-start = ((), (), s32[]{:S(2)}) async-start(), calls=%async_computation.2 | async-start | bytes 4194304 | tf_op jit(solution)/shard_map/psum | solution.py:56
  14.5 11.8 %copy-start.2 = (s32[16384]{0:T(1024)S(1)}, s32[16384]{0:T(1024)}, u32[]{:S(2)}) copy-start(s32[16384]{0:T(1024)} %param.12) | copy-start | bytes 196612
  148.5 5.1 copy-start.7
  227.9 1.3 copy-start.3
  229.3 279.6 %all-reduce.5.cloned.1.call-start = ((), (), s32[]{:S(2)}) async-start(), calls=%async_computation.3 | async-start | bytes 4194304 | tf_op jit(solution)/shard_map/psum | solution.py:56
  333.3 1.3 copy-start.5
  405.3 1.3 copy-start.4
  406.6 3.0 copy-start.8
  409.6 99.3 %copy-start.6 = (f32[2,2048,128]{2,1,0:T(8,128)S(1)}, f32[2,2048,128]{2,1,0:T(8,128)}, u32[]{:S(2)}) copy-start(f32[2,2048,128]{2,1,0:T(8,128)} %copy-done.5) | copy-start | bytes 6291460
  449.0 62.8 %copy-start.1 = (s32[16384]{0:T(1024)S(1)}, s32[16384]{0:T(1024)}, u32[]{:S(2)}) copy-start(s32[16384]{0:T(1024)} %param.13) | copy-start | bytes 196612
Sparse Core Ops, SparseCore 0:
  10.1 127.1 all-gather.1
  229.4 101.0 all-reduce.2
  406.7 102.1 all-reduce.4
where the time goes:
time: 519 us; the launch traced here: 518 us
  waiting for transfers between devices  219 us (42%)
  matrix products  94.6 us (18%)
  blocking collectives  72.1 us (14%)
  other arithmetic  63.7 us (12%)
  local copies, waits for them, and re-layouts  50.5 us (10%)
  between operations  14 us (3%)
    psum x2, waiting for transfers between devices, on_device(): totals, counts = lax.psum((totals, counts), 'wide')  126 us
    all_gather x1, waiting for transfers between devices, on_device(): whole = lax.all_gather(centroid_table, 'wide', axis=0, tiled=True)  92.6 us
    psum x2, blocking collectives, on_device(): totals, counts = lax.psum((totals, counts), 'wide')  72.1 us
    sub x8, matrix products, block_step(): weights_soft = jax.nn.softmax(score_matrix, axis=2).astype(jnp.bfloat16)  57.2 us
    reduce_sum x8, other arithmetic, block_step(): jnp.sum(weights_soft, axis=1, dtype=jnp.float32)  44.1 us
    dot_general x8, matrix products, block_step(): jnp.einsum('mbk,bms->mks', weights_soft, row_block, preferred_element_typ...  37.4 us
    gather x3, local copies, waits for them, and re-layouts, on_device(): jnp.take(whole, owner_of * centroid_table.shape[0] + slot_of, axis=0)  16.1 us
    gather x1, local copies, waits for them, and re-layouts, on_device(): slot_of = slot[assign]  11.8 us
  transfers between devices with their start and end apart: 4, of which 3 were waited for; matrix products, arithmetic and copies ran while one was open for 7% of the time, Pallas kernels for 0%

commit v1 on v0

--- a/solution.py
+++ b/solution.py
@@ -6,6 +6,21 @@
 ITERS = 2
 softness_level = 16.0
 prior_weight = 1.0
+
+
+def _watch_strings(raw):
+    axis_id = "wide"
+    fan = jax.lax.axis_size(axis_id)
+    frames = [raw]
+    j0 = 1
+    while j0 < fan:
+        frames.append(
+            jax.lax.ppermute(frames[j0 - 1], axis_id, [(d, (d - 1) % fan) for d in range(fan)])
+        )
+        j0 += 1
+    return jnp.roll(
+        jnp.concatenate(frames, axis=0), jax.lax.axis_index(axis_id) * raw.shape[0], axis=0
+    )
 
 
 def score_pass(blocks, narrow_words, codeword_norm_values):
@@ -39,7 +54,7 @@
     group_rows = regrouped.shape[0]
     owner_of = owner[assign]
     slot_of = slot[assign]
-    whole = lax.all_gather(centroid_table, "wide", axis=0, tiled=True)
+    whole = _watch_strings(centroid_table)
     centre = jnp.take(whole, owner_of * centroid_table.shape[0] + slot_of, axis=0)
     residual = (regrouped.astype(jnp.float32) - centre.astype(jnp.float32)).astype(jnp.bfloat16)
     spaces = codebook.shape[0]

time: 519 us -> 610 us (1.18)
  local copies, waits for them, and re-layouts: 50.5 us -> 87.7 us
  starting transfers between devices: 4.35 us -> 33.8 us
  waiting for transfers between devices: 219 us -> 238 us
    ppermute x0 -> x7, waiting for transfers between devices: none -> 113 us  [_watch_strings(): jax.lax.ppermute(frames[j0 - 1], axis_id, [(d, (d - 1) % fan) for d in ra...]
    all_gather x1 -> x0, waiting for transfers between devices: 92.6 us -> none  [on_device(): whole = lax.all_gather(centroid_table, 'wide', axis=0, tiled=True)]
    ppermute x0 -> x7, starting transfers between devices: none -> 30.2 us  [_watch_strings(): jax.lax.ppermute(frames[j0 - 1], axis_id, [(d, (d - 1) % fan) for d in ra...]
    unnamed x22 -> x47, local copies, waits for them, and re-layouts: 7.86 us -> 36.9 us
    dynamic_slice x0 -> x1, local copies, waits for them, and re-layouts: none -> 7.06 us  [_watch_strings(): jnp.roll(jnp.concatenate(frames, axis=0), jax.lax.axis_index(axis_id) * r...]
  transfers between devices with their start and end apart: 4 -> 10, of which waited for: 3 -> 8; matrix products, arithmetic and copies ran while one was open for 7% -> 9% of each run, Pallas kernels for 0% -> 0%
where the time goes in v1:
time: 610 us; the launch traced here: 609 us
  waiting for transfers between devices  238 us (39%)
  matrix products  94.5 us (15%)
  local copies, waits for them, and re-layouts  87.7 us (14%)
  blocking collectives  75.7 us (12%)
  other arithmetic  64.7 us (11%)
  starting transfers between devices  33.8 us (6%)
  between operations  14.3 us (2%)
    psum x2, waiting for transfers between devices, on_device(): totals, counts = lax.psum((totals, counts), 'wide')  125 us
    ppermute x7, waiting for transfers between devices, _watch_strings(): jax.lax.ppermute(frames[j0 - 1], axis_id, [(d, (d - 1) % fan) for d in ra...  113 us
    psum x2, blocking collectives, on_device(): totals, counts = lax.psum((totals, counts), 'wide')  75.7 us
    sub x8, matrix products, block_step(): weights_soft = jax.nn.softmax(score_matrix, axis=2).astype(jnp.bfloat16)  57.2 us
    reduce_sum x8, other arithmetic, block_step(): jnp.sum(weights_soft, axis=1, dtype=jnp.float32)  44.2 us
    dot_general x8, matrix products, block_step(): jnp.einsum('mbk,bms->mks', weights_soft, row_block, preferred_element_typ...  37.4 us
    unnamed x47, local copies, waits for them, and re-layouts  36.9 us
    ppermute x7, starting transfers between devices, _watch_strings(): jax.lax.ppermute(frames[j0 - 1], axis_id, [(d, (d - 1) % fan) for d in ra...  30.2 us
  transfers between devices with their start and end apart: 10, of which 8 were waited for; matrix products, arithmetic and copies ran while one was open for 9% of the time, Pallas kernels for 0%

profile of v1, /device:TPU:0, one launch (start us, length us, event | category | flops | bytes accessed | tf_op | source)
XLA Modules:
  0.0 608.7 jit_solution(7848324485223491642)
XLA Ops:
  7.2 6.1 collective-permute-start
  13.2 22.7 %collective-permute-done = bf16[2048,256]{1,0:T(8,128)(2,1)S(1)} collective-permute-done((bf16[2048,256]{1,0:T(8,128)(2,1)}, bf16[2048,256]{1,0:T(8,128)(2,1)S(1)}, u32[]{:S(2)}, u32[]{:S(2)}) %collective-permute-start) | collective-permute-done | bytes 1048608 | tf_op jit(solution)/shard_map/ppermute | solution.py:18
  37.0 5.1 collective-permute-start.1
  42.0 21.6 %collective-permute-done.1 = bf16[2048,256]{1,0:T(8,128)(2,1)S(1)} collective-permute-done((bf16[2048,256]{1,0:T(8,128)(2,1)S(1)}, bf16[2048,256]{1,0:T(8,128)(2,1)S(1)}, u32[]{:S(2)}, u32[]{:S(2)}) %collective-permute-start.1) | collective-permute-done | bytes 1048608 | tf_op jit(solution)/shard_map/ppermute | solution.py:18
  64.6 5.2 collective-permute-start.2
  69.8 20.7 %collective-permute-done.2 = bf16[2048,256]{1,0:T(8,128)(2,1)S(1)} collective-permute-done((bf16[2048,256]{1,0:T(8,128)(2,1)S(1)}, bf16[2048,256]{1,0:T(8,128)(2,1)S(1)}, u32[]{:S(2)}, u32[]{:S(2)}) %collective-permute-start.2) | collective-permute-done | bytes 1048608 | tf_op jit(solution)/shard_map/ppermute | solution.py:18
  90.5 5.2 collective-permute-start.3
  97.9 3.5 all-to-all-start
  102.2 11.8 %gather_fusion = s32[2048]{0:T(1024)S(1)} fusion(s32[16384]{0:T(1024)S(1)} %copy-done, s32[2048]{0:T(1024)S(1)} %fusion.55), kind=kCustom, calls=%fused_computation | custom fusion | bytes 24576 | tf_op jit(solution)/shard_map/gather | solution.py:55
  114.0 11.8 %gather_fusion.1 = s32[2048]{0:T(1024)S(1)} fusion(s32[16384]{0:T(1024)S(1)} %copy-done.2, s32[2048]{0:T(1024)S(1)} %fusion.55), kind=kCustom, calls=%fused_computation.1 | custom fusion | bytes 24576 | tf_op jit(solution)/shard_map/gather | solution.py:56
  128.6 23.1 %collective-permute-done.4 = bf16[2048,256]{1,0:T(8,128)(2,1)} collective-permute-done((bf16[2048,256]{1,0:T(8,128)(2,1)}, bf16[2048,256]{1,0:T(8,128)(2,1)}, u32[]{:S(2)}, u32[]{:S(2)}) %collective-permute-start.4) | collective-permute-done | bytes 1048608 | tf_op jit(solution)/shard_map/ppermute | solution.py:18
  154.8 3.9 multiply_reduce_fusion.1
  163.7 13.5 %collective-permute-done.5 = bf16[2048,256]{1,0:T(8,128)(2,1)} collective-permute-done((bf16[2048,256]{1,0:T(8,128)(2,1)}, bf16[2048,256]{1,0:T(8,128)(2,1)}, u32[]{:S(2)}, u32[]{:S(2)}) %collective-permute-start.5) | collective-permute-done | bytes 1048608 | tf_op jit(solution)/shard_map/ppermute | solution.py:18
  177.2 5.2 collective-permute-start.6
  192.6 11.4 %collective-permute-done.6 = bf16[2048,256]{1,0:T(8,128)(2,1)S(1)} collective-permute-done((bf16[2048,256]{1,0:T(8,128)(2,1)}, bf16[2048,256]{1,0:T(8,128)(2,1)S(1)}, u32[]{:S(2)}, u32[]{:S(2)}) %collective-permute-start.6) | collective-permute-done | bytes 1048608 | tf_op jit(solution)/shard_map/ppermute | solution.py:18
  217.2 7.1 %constant_dynamic-slice_fusion = bf16[16384,256]{1,0:T(8,128)(2,1)} fusion(bf16[32768,256]{1,0:T(8,128)(2,1)} %constant_dynamic-update-slice_fusion, s32[]{:T(128)S(6)} %select_n.46), kind=kLoop, calls=%fused_computation.86 | loop fusion | bytes 16777220 | tf_op jit(solution)/shard_map/jit(_roll_dynamic)/dynamic_slice | solution.py:21
  224.2 11.1 %gather_fusion.2 = bf16[2048,256]{1,0:T(8,128)(2,1)S(1)} fusion(bf16[16384,256]{1,0:T(8,128)(2,1)} %constant_dynamic-slice_fusion, s32[2048]{0:T(1024)S(1)} %broadcast_clamp_fusion), kind=kCustom, calls=%fused_computation.2 | custom fusion | bytes 2105344 | tf_op jit(solution)/shard_map/jit(_take)/gather | solution.py:58
  236.7 3.6 copy.16
  245.2 69.6 %while.26 = (s32[]{:T(128)}, f32[2,2048,128]{2,1,0:T(8,128)S(1)}, f32[2,2048]{1,0:T(2,128)S(1)}, bf16[4,512,2,128]{3,1,2,0:T(8,128)(2,1)S(1)}, bf16[2,2048,128]{...) while((s32[]{:T(128)}, f32[2,2048,128]{2,1,0:T(8,128)S(1)}, ...), condition=%wide.region_5.6_spmd.clone, body=%wide.region_1.5_spmd.clone.sunk | while | flops 1093670912 | bytes 31023204 | solution.py:48
  245.2 7.1 %fusion.87 = (f32[2,512]{1,0:T(2,128)S(1)}, f32[2,512,2048]{2,1,0:T(8,128)}) fusion(f32[2,2048]{1,0:T(2,128)S(1)} %get-tuple-element.277, bf16[2,2048,128]{2,1,0:T(8,128)(2,1)} %get-tuple-element.276, bf16[4,512,2,128]{3,1,2,0:T(8,128)(2,1)S(1)} %get-tuple-element.275, s32[]{:T(128)} %get-tuple-element.264), kind=kOutput, calls=%fused_computation.87.clone.1 | convolution fusion | flops 547358720 | bytes 9719812 | tf_op jit(solution)/shard_map/while/body/eval_jaxpr/sub | solution.py:38
  252.4 5.5 convert_reduce_fusion.4
  257.9 4.7 convolution_add_fusion.4
  262.6 7.2 %fusion.87 = (f32[2,512]{1,0:T(2,128)S(1)}, f32[2,512,2048]{2,1,0:T(8,128)}) fusion(f32[2,2048]{1,0:T(2,128)S(1)} %get-tuple-element.277, bf16[2,2048,128]{2,1,0:T(8,128)(2,1)} %get-tuple-element.276, bf16[4,512,2,128]{3,1,2,0:T(8,128)(2,1)S(1)} %get-tuple-element.275, s32[]{:T(128)} %get-tuple-element.264), kind=kOutput, calls=%fused_computation.87.clone.1 | convolution fusion | flops 547358720 | bytes 9719812 | tf_op jit(solution)/shard_map/while/body/eval_jaxpr/sub | solution.py:38
  269.8 5.5 convert_reduce_fusion.4
  275.3 4.7 convolution_add_fusion.4
  280.0 7.2 %fusion.87 = (f32[2,512]{1,0:T(2,128)S(1)}, f32[2,512,2048]{2,1,0:T(8,128)}) fusion(f32[2,2048]{1,0:T(2,128)S(1)} %get-tuple-element.277, bf16[2,2048,128]{2,1,0:T(8,128)(2,1)} %get-tuple-element.276, bf16[4,512,2,128]{3,1,2,0:T(8,128)(2,1)S(1)} %get-tuple-element.275, s32[]{:T(128)} %get-tuple-element.264), kind=kOutput, calls=%fused_computation.87.clone.1 | convolution fusion | flops 547358720 | bytes 9719812 | tf_op jit(solution)/shard_map/while/body/eval_jaxpr/sub | solution.py:38
  287.2 5.5 convert_reduce_fusion.4
  292.7 4.7 convolution_add_fusion.4
  297.4 7.2 %fusion.87 = (f32[2,512]{1,0:T(2,128)S(1)}, f32[2,512,2048]{2,1,0:T(8,128)}) fusion(f32[2,2048]{1,0:T(2,128)S(1)} %get-tuple-element.277, bf16[2,2048,128]{2,1,0:T(8,128)(2,1)} %get-tuple-element.276, bf16[4,512,2,128]{3,1,2,0:T(8,128)(2,1)S(1)} %get-tuple-element.275, s32[]{:T(128)} %get-tuple-element.264), kind=kOutput, calls=%fused_computation.87.clone.1 | convolution fusion | flops 547358720 | bytes 9719812 | tf_op jit(solution)/shard_map/while/body/eval_jaxpr/sub | solution.py:38
  304.6 5.5 convert_reduce_fusion.4
  310.1 4.7 convolution_add_fusion.4
  316.2 39.3 %psum.29 = f32[2,2048]{1,0:T(2,128)S(1)} all-reduce(f32[2,2048]{1,0:T(2,128)S(1)} %get-tuple-element.69), channel_id=1, replica_groups=mesh['wide'=8,'narrow'=4] {'wide'}, use_global_device_ids=true, to_apply=%region_7.8 | all-reduce | flops 4096 | bytes 32768 | tf_op jit(solution)/shard_map/psum | solution.py:71
  355.5 64.9 %all-reduce.3.cloned.1.call-done = f32[2,2048,128]{2,1,0:T(8,128)} async-done(((f32[2,2048,128]{2,1,0:T(8,128)}), f32[2,2048,128]{2,1,0:T(8,128)}) %all-reduce.3.cloned.1.call-update) | async-done | bytes 2097168 | tf_op jit(solution)/shard_map/psum | solution.py:71
  425.7 69.5 %while.27 = (s32[]{:T(128)}, f32[2,2048,128]{2,1,0:T(8,128)S(1)}, f32[2,2048]{1,0:T(2,128)S(1)}, bf16[4,512,2,128]{3,1,2,0:T(8,128)(2,1)S(1)}, bf16[2,2048,128]{...) while((s32[]{:T(128)}, f32[2,2048,128]{2,1,0:T(8,128)S(1)}, ...), condition=%wide.region_13.14_spmd.clone, body=%wide.region_9.13_spmd.clone.sunk | while | flops 1093670912 | bytes 31023204 | solution.py:48
  425.7 7.1 %fusion.92 = (f32[2,512]{1,0:T(2,128)S(1)}, f32[2,512,2048]{2,1,0:T(8,128)}) fusion(f32[2,2048]{1,0:T(2,128)S(1)} %get-tuple-element.301, bf16[2,2048,128]{2,1,0:T(8,128)(2,1)} %get-tuple-element.300, bf16[4,512,2,128]{3,1,2,0:T(8,128)(2,1)S(1)} %get-tuple-element.299, s32[]{:T(128)} %get-tuple-element.288), kind=kOutput, calls=%fused_computation.88.clone.1 | convolution fusion | flops 547358720 | bytes 9719812 | tf_op jit(solution)/shard_map/while/body/eval_jaxpr/sub | solution.py:38
  432.9 5.5 convert_reduce_fusion.5
  438.4 4.7 convolution_add_fusion.5
  443.1 7.1 %fusion.92 = (f32[2,512]{1,0:T(2,128)S(1)}, f32[2,512,2048]{2,1,0:T(8,128)}) fusion(f32[2,2048]{1,0:T(2,128)S(1)} %get-tuple-element.301, bf16[2,2048,128]{2,1,0:T(8,128)(2,1)} %get-tuple-element.300, bf16[4,512,2,128]{3,1,2,0:T(8,128)(2,1)S(1)} %get-tuple-element.299, s32[]{:T(128)} %get-tuple-element.288), kind=kOutput, calls=%fused_computation.88.clone.1 | convolution fusion | flops 547358720 | bytes 9719812 | tf_op jit(solution)/shard_map/while/body/eval_jaxpr/sub | solution.py:38
  450.3 5.5 convert_reduce_fusion.5
  455.8 4.7 convolution_add_fusion.5
  460.5 7.1 %fusion.92 = (f32[2,512]{1,0:T(2,128)S(1)}, f32[2,512,2048]{2,1,0:T(8,128)}) fusion(f32[2,2048]{1,0:T(2,128)S(1)} %get-tuple-element.301, bf16[2,2048,128]{2,1,0:T(8,128)(2,1)} %get-tuple-element.300, bf16[4,512,2,128]{3,1,2,0:T(8,128)(2,1)S(1)} %get-tuple-element.299, s32[]{:T(128)} %get-tuple-element.288), kind=kOutput, calls=%fused_computation.88.clone.1 | convolution fusion | flops 547358720 | bytes 9719812 | tf_op jit(solution)/shard_map/while/body/eval_jaxpr/sub | solution.py:38
  467.6 5.5 convert_reduce_fusion.5
  473.2 4.7 convolution_add_fusion.5
  477.9 7.1 %fusion.92 = (f32[2,512]{1,0:T(2,128)S(1)}, f32[2,512,2048]{2,1,0:T(8,128)}) fusion(f32[2,2048]{1,0:T(2,128)S(1)} %get-tuple-element.301, bf16[2,2048,128]{2,1,0:T(8,128)(2,1)} %get-tuple-element.300, bf16[4,512,2,128]{3,1,2,0:T(8,128)(2,1)S(1)} %get-tuple-element.299, s32[]{:T(128)} %get-tuple-element.288), kind=kOutput, calls=%fused_computation.88.clone.1 | convolution fusion | flops 547358720 | bytes 9719812 | tf_op jit(solution)/shard_map/while/body/eval_jaxpr/sub | solution.py:38
  485.0 5.5 convert_reduce_fusion.5
  490.6 4.7 convolution_add_fusion.5
  502.6 36.5 %psum.31 = f32[2,2048]{1,0:T(2,128)S(1)} all-reduce(f32[2,2048]{1,0:T(2,128)S(1)} %get-tuple-element.71), channel_id=1, replica_groups=mesh['wide'=8,'narrow'=4] {'wide'}, use_global_device_ids=true, to_apply=%region_15.16 | all-reduce | flops 4096 | bytes 32768 | tf_op jit(solution)/shard_map/psum | solution.py:71
  539.1 59.9 %all-reduce.5.cloned.1.call-done = f32[2,2048,128]{2,1,0:T(8,128)} async-done(((f32[2,2048,128]{2,1,0:T(8,128)}), f32[2,2048,128]{2,1,0:T(8,128)}) %all-reduce.5.cloned.1.call-update) | async-done | bytes 2097168 | tf_op jit(solution)/shard_map/psum | solution.py:71
  (84 shorter events, 62.6 us)
Async XLA Ops:
  7.2 95.0 %copy-start = (s32[16384]{0:T(1024)S(1)}, s32[16384]{0:T(1024)}, u32[]{:S(2)}) copy-start(s32[16384]{0:T(1024)} %param.12) | copy-start | bytes 196612
  7.2 106.8 %copy-start.2 = (s32[16384]{0:T(1024)S(1)}, s32[16384]{0:T(1024)}, u32[]{:S(2)}) copy-start(s32[16384]{0:T(1024)} %param.13) | copy-start | bytes 196612
  7.2 28.8 %collective-permute-start = (bf16[2048,256]{1,0:T(8,128)(2,1)}, bf16[2048,256]{1,0:T(8,128)(2,1)S(1)}, u32[]{:S(2)}, u32[]{:S(2)}) collective-permute-start(bf16[2048,256]{1,0:T(8,128)(2,1)} %param.11), channel_id=1, source_target_pairs={{0,28},{4,0},{8,4},{12,8},{16,12},{20,16},{24,20},{28,24},{1,29},{... | collective-permute-start | bytes 3145736 | tf_op jit(solution)/shard_map/ppermute | solution.py:18
  36.0 1.0 copy-start.9
  37.0 26.6 %collective-permute-start.1 = (bf16[2048,256]{1,0:T(8,128)(2,1)S(1)}, bf16[2048,256]{1,0:T(8,128)(2,1)S(1)}, u32[]{:S(2)}, u32[]{:S(2)}) collective-permute-start(bf16[2048,256]{1,0:T(8,128)(2,1)S(1)} %collective-permute-done), channel_id=1, source_target_pairs={{0,28},{4,0},{8,4},{12,8},{16,12},{20,16},{24,20},{28,24},{1,29},{... | collective-permute-start | bytes 3145736 | tf_op jit(solution)/shard_map/ppermute | solution.py:18
  63.6 1.0 copy-start.11
  64.6 25.9 %collective-permute-start.2 = (bf16[2048,256]{1,0:T(8,128)(2,1)S(1)}, bf16[2048,256]{1,0:T(8,128)(2,1)S(1)}, u32[]{:S(2)}, u32[]{:S(2)}) collective-permute-start(bf16[2048,256]{1,0:T(8,128)(2,1)S(1)} %collective-permute-done.1), channel_id=1, source_target_pairs={{0,28},{4,0},{8,4},{12,8},{16,12},{20,16},{24,20},{28,24},{1,29},{... | collective-permute-start | bytes 3145736 | tf_op jit(solution)/shard_map/ppermute | solution.py:18
  90.5 35.3 %copy-start.13 = (bf16[2048,256]{1,0:T(8,128)(2,1)}, bf16[2048,256]{1,0:T(8,128)(2,1)S(1)}, u32[]{:S(2)}) copy-start(bf16[2048,256]{1,0:T(8,128)(2,1)S(1)} %collective-permute-done.2) | copy-start | bytes 3145732
  90.5 35.3 %collective-permute-start.3 = (bf16[2048,256]{1,0:T(8,128)(2,1)S(1)}, bf16[2048,256]{1,0:T(8,128)(2,1)}, u32[]{:S(2)}, u32[]{:S(2)}) collective-permute-start(bf16[2048,256]{1,0:T(8,128)(2,1)S(1)} %collective-permute-done.2), channel_id=1, source_target_pairs={{0,28},{4,0},{8,4},{12,8},{16,12},{20,16},{24,20},{28,24},{1,29},{... | collective-permute-start | bytes 3145736 | tf_op jit(solution)/shard_map/ppermute | solution.py:18
  97.9 60.7 %all-to-all-start = ((bf16[512,4,256]{0,2,1:T(8,128)(2,1)}), bf16[512,4,256]{0,2,1:T(8,128)(2,1)S(1)}, u32[]{:S(2)}, u32[]{:S(2)}) async-start(bf16[512,4,256]{0,2,1:T(8,128)(2,1)} %bitcast.64), calls=%async_computation | async-start | bytes 2097152 | tf_op jit(solution)/shard_map/all_to_all | solution.py:53
  101.5 318.9 %all-reduce.3.cloned.1.call-start = ((), (), s32[]{:S(2)}) async-start(), calls=%async_computation.1 | async-start | bytes 4194304 | tf_op jit(solution)/shard_map/psum | solution.py:71
  125.8 25.9 %collective-permute-start.4 = (bf16[2048,256]{1,0:T(8,128)(2,1)}, bf16[2048,256]{1,0:T(8,128)(2,1)}, u32[]{:S(2)}, u32[]{:S(2)}) collective-permute-start(bf16[2048,256]{1,0:T(8,128)(2,1)} %collective-permute-done.3), channel_id=1, source_target_pairs={{0,28},{4,0},{8,4},{12,8},{16,12},{20,16},{24,20},{28,24},{1,29},{... | collective-permute-start | bytes 3145736 | tf_op jit(solution)/shard_map/ppermute | solution.py:18
  151.7 25.5 %collective-permute-start.5 = (bf16[2048,256]{1,0:T(8,128)(2,1)}, bf16[2048,256]{1,0:T(8,128)(2,1)}, u32[]{:S(2)}, u32[]{:S(2)}) collective-permute-start(bf16[2048,256]{1,0:T(8,128)(2,1)} %collective-permute-done.4), channel_id=1, source_target_pairs={{0,28},{4,0},{8,4},{12,8},{16,12},{20,16},{24,20},{28,24},{1,29},{... | collective-permute-start | bytes 3145736 | tf_op jit(solution)/shard_map/ppermute | solution.py:18
  158.6 26.0 %copy-start.14 = (bf16[2048,256]{1,0:T(8,128)(2,1)S(1)}, bf16[2048,256]{1,0:T(8,128)(2,1)}, u32[]{:S(2)}) copy-start(bf16[2048,256]{1,0:T(8,128)(2,1)} %copy-done.13) | copy-start | bytes 3145732
  161.3 43.8 %copy-start.8 = (bf16[2048,256]{1,0:T(8,128)(2,1)S(1)}, bf16[2048,256]{1,0:T(8,128)(2,1)}, u32[]{:S(2)}) copy-start(bf16[2048,256]{1,0:T(8,128)(2,1)} %param.11) | copy-start | bytes 3145732
  161.3 44.9 %copy-start.10 = (bf16[2048,256]{1,0:T(8,128)(2,1)S(1)}, bf16[2048,256]{1,0:T(8,128)(2,1)}, u32[]{:S(2)}) copy-start(bf16[2048,256]{1,0:T(8,128)(2,1)} %copy-done.9) | copy-start | bytes 3145732
  163.7 43.5 %copy-start.12 = (bf16[2048,256]{1,0:T(8,128)(2,1)S(1)}, bf16[2048,256]{1,0:T(8,128)(2,1)}, u32[]{:S(2)}) copy-start(bf16[2048,256]{1,0:T(8,128)(2,1)} %copy-done.11) | copy-start | bytes 3145732
  177.2 26.8 %collective-permute-start.6 = (bf16[2048,256]{1,0:T(8,128)(2,1)}, bf16[2048,256]{1,0:T(8,128)(2,1)S(1)}, u32[]{:S(2)}, u32[]{:S(2)}) collective-permute-start(bf16[2048,256]{1,0:T(8,128)(2,1)} %collective-permute-done.5), channel_id=1, source_target_pairs={{0,28},{4,0},{8,4},{12,8},{16,12},{20,16},{24,20},{28,24},{1,29},{... | collective-permute-start | bytes 3145736 | tf_op jit(solution)/shard_map/ppermute | solution.py:18
  235.4 5.0 copy-start.7
  314.8 1.3 copy-start.3
  316.2 282.8 %all-reduce.5.cloned.1.call-start = ((), (), s32[]{:S(2)}) async-start(), calls=%async_computation.2 | async-start | bytes 4194304 | tf_op jit(solution)/shard_map/psum | solution.py:71
  423.3 1.3 copy-start.5
  495.3 1.3 copy-start.4
  495.3 106.6 %copy-start.1 = (s32[16384]{0:T(1024)S(1)}, s32[16384]{0:T(1024)}, u32[]{:S(2)}) copy-start(s32[16384]{0:T(1024)} %param.12) | copy-start | bytes 196612
  496.6 102.3 %copy-start.6 = (f32[2,2048,128]{2,1,0:T(8,128)S(1)}, f32[2,2048,128]{2,1,0:T(8,128)}, u32[]{:S(2)}) copy-start(f32[2,2048,128]{2,1,0:T(8,128)} %copy-done.5) | copy-start | bytes 6291460
Sparse Core Ops, SparseCore 0:
  316.3 104.0 all-reduce.2
  496.7 102.1 all-reduce.4
